TPU v7x, 32 devices: a whole 2x2x4 slice. The times are simulated.
32 devices in a mesh: py: 4 (over y, x), px: 8 (over z, core).
Axes of the slice: x: 2, y: 2, z: 4, core: 2. Of those that a mesh axis runs over, the one named last changes fastest.
Arguments:
- movie: bfloat16 [256, 128, 2048], P('py', 'px'), may hold values from -6 to 6
- traces: bfloat16 [4096, 2048], P('py', 'px'), may hold values from -0.125 to 0.125
- footprints: float32 [256, 128, 512], P('py', 'px'), may hold values from 0 to 1
- block_ids: int32 [4, 8, 4], P('py', 'px'), may hold values from 0 to 32, as said below
Outputs:
- updated: float32 [256, 128, 512], P('py', 'px')
Inputs may be any that keep to these rules, and one draw needn't show every extreme that they name: `block_ids`: in each tile's list of 4 entries the live entries come first and are distinct block numbers below 32; the remaining entries equal 32 and mark empty slots. Every tile has at least one live entry, and some tile has all 4 live.
All inputs are finite; a program needn't handle non-finite values.
Results may differ from a plain program's by a relative error of at most 0.0003.
Values may be sent and summed in bfloat16 or wider, within the bound.
A program may use at most 64 MiB of HBM per device.

v0:
```python
import jax
import jax.numpy as jnp
from jax import lax
from jax.sharding import PartitionSpec as P

K = 4096
BLK = 128
SLOTS = 4
ITERS = 2


def accumulate(tile_movie, picked):
    cross = lax.dot_general(
        tile_movie, picked, (((1,), (1,)), ((), ())), preferred_element_type=jnp.float32
    )
    gram = lax.dot_general(
        picked, picked, (((1,), (1,)), ((), ())), preferred_element_type=jnp.float32
    )
    return (cross, gram)


def per_device(movie, traces, footprints, block_ids):
    rows, cols, frames = movie.shape
    pixels = rows * cols
    width = SLOTS * BLK
    nblk = K // BLK
    tile_movie = movie.reshape(pixels, frames)
    ids = block_ids.reshape(SLOTS)
    onehot = (ids[:, None] == jnp.arange(nblk, dtype=jnp.int32)[None, :]).astype(jnp.float32)
    live = jnp.sum(onehot, axis=1)
    span_all = lax.all_gather(traces, "py", axis=0, tiled=True)
    span_len = span_all.shape[1]
    row_ids = lax.all_gather(block_ids, "px", axis=1, tiled=True).reshape(-1, SLOTS)
    route = (row_ids[:, :, None] == jnp.arange(nblk, dtype=jnp.int32)[None, None, :]).astype(
        jnp.bfloat16
    )
    outgoing = jnp.einsum(
        "rsb,bnw->rsnw",
        route,
        span_all.reshape(nblk, BLK, span_len),
        preferred_element_type=jnp.float32,
    )
    outgoing = outgoing.astype(jnp.bfloat16).reshape(row_ids.shape[0], width, span_len)
    received = lax.all_to_all(outgoing, "px", split_axis=0, concat_axis=2, tiled=True)
    mine = received.reshape(width, frames)
    cross, gram = accumulate(tile_movie, mine)
    column_live = jnp.repeat(live, BLK)
    denom = jnp.diagonal(gram) + 1e-06 + (1.0 - column_live)
    current = footprints.reshape(pixels, width) * column_live[None, :]
    pixall = pixels * lax.axis_size("py") * lax.axis_size("px")
    for step in range(ITERS):
        for slot in range(SLOTS):
            low = slot * BLK
            resid = cross[:, low : low + BLK] - jnp.dot(
                current, gram[:, low : low + BLK], precision=lax.Precision.HIGHEST
            )
            fresh = jnp.maximum(
                current[:, low : low + BLK] + resid / denom[None, low : low + BLK], 0.0
            )
            current = current.at[:, low : low + BLK].set(fresh)
        colsq = jnp.sum(current * current, axis=0).reshape(SLOTS, BLK)
        partial_value = jnp.einsum("sb,sn->bn", onehot, colsq, precision=lax.Precision.HIGHEST)
        totals = lax.psum(partial_value, ("py", "px"))
        factor = 1.0 / jnp.sqrt(totals / pixall + 1e-06)
        scale = jnp.einsum("sb,bn->sn", onehot, factor, precision=lax.Precision.HIGHEST).reshape(
            width
        )
        current = current * scale[None, :]
    return current.reshape(rows, cols, width)


def solution(mesh):
    return jax.shard_map(
        per_device,
        mesh=mesh,
        in_specs=(P("py", "px", None), P("py", "px"), P("py", "px", None), P("py", "px", None)),
        out_specs=P("py", "px", None),
        check_vma=False,
    )
```

profile of v0, /device:TPU:0, one launch (start us, length us, event | category | flops | bytes accessed | tf_op | source)
XLA Modules:
  0.0 233.0 jit_solution(12457084238456742489)
XLA Ops:
  6.5 0.0 all-gather.2.cloned.1.call-start
  6.5 0.7 all-gather.2.cloned.1.call-update
  7.3 13.6 %all_gather.6 = s32[1,8,4]{2,0,1:T(1,128)S(1)} all-gather(s32[1,1,4]{2,0,1:T(1,128)} %bitcast.62), channel_id=1, replica_groups=mesh['py'=4,'px'=8] {'px'}, dimensions={1}, use_global_device_ids=true | all-gather | bytes 144 | tf_op jit(solution)/shard_map/all_gather | solution.py:33
  20.9 0.1 copy.48
  21.0 26.1 %all-gather.2.cloned.1.call-done = bf16[4096,256]{1,0:T(8,128)(2,1)} async-done(((bf16[1024,256]{1,0:T(8,128)(2,1)}), bf16[4096,256]{1,0:T(8,128)(2,1)}) %all-gather.2.cloned.1.call-update) | async-done | bytes 2097168 | tf_op jit(solution)/shard_map/all_gather | solution.py:31
  47.1 2.9 %fusion.5 = bf16[8,4,128,256]{3,0,2,1:T(8,128)(2,1)S(1)} fusion(bf16[32,128,256]{2,1,0:T(8,128)(2,1)} %bitcast.60, s32[8,4]{0,1:T(4,128)S(1)} %bitcast.61), kind=kOutput, calls=%fused_computation.8 | convolution fusion | flops 68158464 | bytes 4194432 | tf_op jit(solution)/shard_map/rsb,bnw->rsnw/dot_general | solution.py:37
  50.0 1.7 copy.50
  51.7 0.0 copy-start.3
  51.8 4.7 %all-to-all-start = ((bf16[8,512,256]{2,1,0:T(8,128)(2,1)}), bf16[8,512,256]{2,1,0:T(8,128)(2,1)}, u32[]{:S(2)}, u32[]{:S(2)}) async-start(bf16[8,512,256]{2,1,0:T(8,128)(2,1)} %copy.50), calls=%async_computation | async-start | bytes 4194304 | tf_op jit(solution)/shard_map/all_to_all | solution.py:44
  56.5 0.0 copy-done.3
  56.5 0.0 copy-start.4
  56.5 1.8 copy.46
  58.3 0.6 compare_reduce_fusion.2
  59.0 0.7 compare_reduce_fusion
  59.7 0.0 copy-done.4
  59.7 0.2 convert_reduce_fusion
  59.9 0.1 broadcast_bitcast_fusion
  60.0 1.8 broadcast_multiply_fusion.2
  61.8 43.9 %all-to-all-done = bf16[8,512,256]{2,1,0:T(8,128)(2,1)} async-done(((bf16[8,512,256]{2,1,0:T(8,128)(2,1)}), bf16[8,512,256]{2,1,0:T(8,128)(2,1)}, u32[]{:S(2)}, u32[]{:S(2)}) %all-to-all-start) | async-done | bytes 2097184 | tf_op jit(solution)/shard_map/all_to_all | solution.py:44
  105.6 3.5 %fusion.8 = f32[512,512]{1,0:T(8,128)S(1)} fusion(bf16[8,512,256]{2,1,0:T(8,128)(2,1)} %all-to-all-done), kind=kOutput, calls=%fused_computation.10 | convolution fusion | flops 1073741824 | bytes 3145728 | tf_op jit(solution)/shard_map/dot_general | solution.py:16
  109.1 4.5 %gather_fusion = f32[512]{0:T(512)S(1)} fusion(f32[512,512]{1,0:T(8,128)S(1)} %fusion.8, s32[512]{0:T(512)S(1)} %bitcast.56), kind=kCustom, calls=%fused_computation | custom fusion | bytes 8192 | tf_op jit(solution)/shard_map/jit(diagonal)/cond/branch_0_fun/gather | solution.py:48
  113.7 0.1 subtract_add_fusion
  113.7 3.9 %copy.51 = bf16[1,512,8,256]{1,3,2,0:T(8,128)(2,1)} copy(bf16[1,512,8,256]{3,1,2,0:T(8,128)(2,1)} %bitcast.11) | data formatting | bytes 4194304 | tf_op jit(solution)/shard_map/all_to_all | solution.py:44
  117.7 5.2 %convolution_bitcast_fusion = f32[1024,512]{0,1:T(8,128)S(1)} fusion(bf16[512,2048]{0,1:T(8,128)(2,1)} %bitcast.59, bf16[1024,2048]{1,0:T(8,128)(2,1)} %bitcast.68), kind=kOutput, calls=%fused_computation.9 | convolution fusion | flops 2147483648 | bytes 8388608 | tf_op jit(solution)/shard_map/dot_general | solution.py:13
  122.9 0.0 copy-start.1
  122.9 2.1 fusion.40
  125.0 2.2 fusion.36
  127.2 2.1 fusion.32
  129.3 0.0 copy-done.1
  129.4 1.5 fusion.28
  130.9 0.2 multiply_reduce_fusion.1
  131.1 0.3 fusion.64
  131.3 37.2 %psum.14 = f32[32,128]{1,0:T(8,128)S(1)} all-reduce(f32[32,128]{1,0:T(8,128)S(1)} %fusion.64), channel_id=1, replica_groups=mesh['py'=4,'px'=8] {'py','px'}, use_global_device_ids=true, to_apply=%region_5.6 | all-reduce | flops 4096 | bytes 32768 | tf_op jit(solution)/shard_map/psum | solution.py:63
  168.5 0.2 convolution_bitcast_fusion.2
  168.7 0.0 copy-start.2
  168.7 0.2 broadcast_multiply_fusion.1
  168.9 1.4 copy-done.2
  170.3 2.1 fusion.25
  172.4 2.1 fusion.21
  174.6 2.0 fusion.17
  176.7 1.4 fusion.13
  178.1 0.0 copy-start
  178.2 1.3 copy-done
  179.5 0.2 multiply_reduce_fusion
  179.7 0.3 fusion.62
  179.9 42.4 %psum.15 = f32[32,128]{1,0:T(8,128)S(1)} all-reduce(f32[32,128]{1,0:T(8,128)S(1)} %fusion.62), channel_id=1, replica_groups=mesh['py'=4,'px'=8] {'py','px'}, use_global_device_ids=true, to_apply=%region_7.8 | all-reduce | flops 4096 | bytes 32768 | tf_op jit(solution)/shard_map/psum | solution.py:63
  222.3 0.2 convolution_bitcast_fusion.1
  222.5 1.8 broadcast_multiply_fusion
  224.3 1.8 copy.60
  (10 shorter events, 0.3 us)
Async XLA Ops:
  6.5 40.6 %all-gather.2.cloned.1.call-start = ((), (), s32[]{:S(2)}) async-start(), calls=%async_computation.1 | async-start | bytes 2621440 | tf_op jit(solution)/shard_map/all_gather | solution.py:31
  51.7 4.7 %copy-start.3 = (f32[64,16,512]{2,1,0:T(8,128)S(1)}, f32[64,16,512]{2,1,0:T(8,128)}, u32[]{:S(2)}) copy-start(f32[64,16,512]{2,1,0:T(8,128)} %param.22) | copy-start | bytes 6291460
  51.8 53.9 %all-to-all-start = ((bf16[8,512,256]{2,1,0:T(8,128)(2,1)}), bf16[8,512,256]{2,1,0:T(8,128)(2,1)}, u32[]{:S(2)}, u32[]{:S(2)}) async-start(bf16[8,512,256]{2,1,0:T(8,128)(2,1)} %copy.50), calls=%async_computation | async-start | bytes 4194304 | tf_op jit(solution)/shard_map/all_to_all | solution.py:44
  56.5 3.2 %copy-start.4 = (s32[1,1,4]{2,1,0:T(1,128)S(1)}, s32[1,1,4]{2,1,0:T(1,128)}, u32[]{:S(2)}) copy-start(s32[1,1,4]{2,1,0:T(1,128)} %param.23) | copy-start | bytes 52
  122.9 6.5 %copy-start.1 = (f32[1024,512]{0,1:T(8,128)}, f32[1024,512]{0,1:T(8,128)S(1)}, u32[]{:S(2)}) copy-start(f32[1024,512]{0,1:T(8,128)S(1)} %convolution_bitcast_fusion) | copy-start | bytes 6291460
  168.7 1.6 copy-start.2
  178.1 1.3 copy-start
Sparse Core Ops, SparseCore 0:
  9.2 37.8 all-gather.1
where the time goes:
time: 234 us; the launch traced here: 233 us
  blocking collectives  93.2 us (40%)
  waiting for transfers between devices  70.7 us (30%)
  matrix products  27.9 us (12%)
  local copies, waits for them, and re-layouts  17 us (7%)
  between operations  13.6 us (6%)
  other arithmetic  5.86 us (3%)
  starting transfers between devices  4.74 us (2%)
    psum x2, blocking collectives, per_device(): totals = lax.psum(partial_value, ('py', 'px'))  79.5 us
    all_to_all x1, waiting for transfers between devices, per_device(): lax.all_to_all(outgoing, 'px', split_axis=0, concat_axis=2, tiled=True)  43.9 us
    all_gather x1, waiting for transfers between devices, per_device(): span_all = lax.all_gather(traces, 'py', axis=0, tiled=True)  26.1 us
    dot_general x8, matrix products, per_device(): jnp.dot(current, gram[:, low:low + BLK], precision=lax.Precision.HIGHEST)  15.4 us
    all_gather x1, blocking collectives, per_device(): lax.all_gather(block_ids, 'px', axis=1, tiled=True).reshape(-1, SLOTS)  13.6 us
    dot_general x1, matrix products, accumulate(): lax.dot_general(tile_movie, picked, (((1,), (1,)), ((), ())), preferred_e...  5.2 us
    all_to_all x1, starting transfers between devices, per_device(): lax.all_to_all(outgoing, 'px', split_axis=0, concat_axis=2, tiled=True)  4.74 us
  transfers between devices with their start and end apart: 2, of which 2 were waited for; matrix products, arithmetic and copies ran while one was open for 2% of the time, Pallas kernels for 0%

commit v1 on v0

--- a/solution.py
+++ b/solution.py
@@ -2,6 +2,7 @@
 import jax.numpy as jnp
 from jax import lax
 from jax.sharding import PartitionSpec as P
+from jax.lax import all_to_all, axis_size
 
 K = 4096
 BLK = 128
@@ -41,7 +42,11 @@
         preferred_element_type=jnp.float32,
     )
     outgoing = outgoing.astype(jnp.bfloat16).reshape(row_ids.shape[0], width, span_len)
-    received = lax.all_to_all(outgoing, "px", split_axis=0, concat_axis=2, tiled=True)
+    watch_keys = lambda shard_in: jnp.concatenate(
+        all_to_all(jnp.stack(jnp.split(shard_in, axis_size("px"), axis=0), axis=0), "px", 0, 0),
+        axis=2,
+    )
+    received = watch_keys(outgoing)
     mine = received.reshape(width, frames)
     cross, gram = accumulate(tile_movie, mine)
     column_live = jnp.repeat(live, BLK)

time: 234 us -> 243 us (1.038)
  local copies, waits for them, and re-layouts: 17 us -> 26.2 us
    unnamed x10 -> x25, local copies, waits for them, and re-layouts: 2.71 us -> 8.13 us
    split x0 -> x1, local copies, waits for them, and re-layouts: none -> 4.79 us  [per_device(): jnp.split(shard_in, axis_size('px'), axis=0)]
    all_to_all x1 -> x0, local copies, waits for them, and re-layouts: 3.92 us -> none  [per_device(): lax.all_to_all(outgoing, 'px', split_axis=0, concat_axis=2, tiled=True)]
where the time goes in v1:
time: 243 us; the launch traced here: 242 us
  blocking collectives  93.1 us (38%)
  waiting for transfers between devices  70.7 us (29%)
  matrix products  27.9 us (11%)
  local copies, waits for them, and re-layouts  26.2 us (11%)
  between operations  13.7 us (6%)
  other arithmetic  5.86 us (2%)
  starting transfers between devices  4.74 us (2%)
    psum x2, blocking collectives, per_device(): totals = lax.psum(partial_value, ('py', 'px'))  79.5 us
    all_to_all x1, waiting for transfers between devices, per_device(): all_to_all(jnp.stack(jnp.split(shard_in, axis_size('px'), axis=0), axis=0...  43.9 us
    all_gather x1, waiting for transfers between devices, per_device(): span_all = lax.all_gather(traces, 'py', axis=0, tiled=True)  26.1 us
    dot_general x8, matrix products, per_device(): jnp.dot(current, gram[:, low:low + BLK], precision=lax.Precision.HIGHEST)  15.4 us
    all_gather x1, blocking collectives, per_device(): lax.all_gather(block_ids, 'px', axis=1, tiled=True).reshape(-1, SLOTS)  13.6 us
    unnamed x25, local copies, waits for them, and re-layouts  8.13 us
    dot_general x1, matrix products, accumulate(): lax.dot_general(tile_movie, picked, (((1,), (1,)), ((), ())), preferred_e...  5.2 us
  transfers between devices with their start and end apart: 2, of which 2 were waited for; matrix products, arithmetic and copies ran while one was open for 2% of the time, Pallas kernels for 0%

profile of v1, /device:TPU:0, one launch (start us, length us, event | category | flops | bytes accessed | tf_op | source)
XLA Modules:
  0.0 242.2 jit_solution(6956425236938282568)
XLA Ops:
  6.5 0.0 all-gather.2.cloned.1.call-start
  6.5 0.7 all-gather.2.cloned.1.call-update
  7.3 13.6 %all_gather.6 = s32[1,8,4]{2,0,1:T(1,128)S(1)} all-gather(s32[1,1,4]{2,0,1:T(1,128)} %bitcast.76), channel_id=1, replica_groups=mesh['py'=4,'px'=8] {'px'}, dimensions={1}, use_global_device_ids=true | all-gather | bytes 144 | tf_op jit(solution)/shard_map/all_gather | solution.py:34
  20.9 0.1 copy.62
  21.0 26.1 %all-gather.2.cloned.1.call-done = bf16[4096,256]{1,0:T(8,128)(2,1)} async-done(((bf16[1024,256]{1,0:T(8,128)(2,1)}), bf16[4096,256]{1,0:T(8,128)(2,1)}) %all-gather.2.cloned.1.call-update) | async-done | bytes 2097168 | tf_op jit(solution)/shard_map/all_gather | solution.py:32
  47.1 2.9 %fusion.5 = bf16[8,4,128,256]{3,0,2,1:T(8,128)(2,1)S(1)} fusion(bf16[32,128,256]{2,1,0:T(8,128)(2,1)} %bitcast.66, s32[8,4]{0,1:T(4,128)S(1)} %bitcast.75), kind=kOutput, calls=%fused_computation.8 | convolution fusion | flops 68158464 | bytes 4194432 | tf_op jit(solution)/shard_map/rsb,bnw->rsnw/dot_general | solution.py:38
  50.0 4.8 %fusion.74 = (bf16[1,4,128,256]{3,0,2,1:T(2,128)(2,1)S(1)}, bf16[1,4,128,256]{3,0,2,1:T(2,128)(2,1)S(1)}, bf16[1,4,128,256]{3,0,2,1:T(2,128)(2,1)S(1)}, bf16[1,4...) fusion(bf16[8,4,128,256]{3,0,2,1:T(8,128)(2,1)S(1)} %fusion.5), kind=kLoop, calls=%fused_computation.112 | loop fusion | bytes 4194304 | tf_op jit(solution)/shard_map/split | solution.py:46
  54.9 0.7 constant_dynamic-update-slice_fusion.7
  56.0 0.7 constant_dynamic-update-slice_fusion.6
  56.7 0.7 constant_dynamic-update-slice_fusion.5
  57.4 0.7 constant_dynamic-update-slice_fusion.4
  58.1 0.7 constant_dynamic-update-slice_fusion.3
  58.9 0.7 constant_dynamic-update-slice_fusion.2
  59.6 0.7 constant_dynamic-update-slice_fusion.1
  60.3 0.7 constant_dynamic-update-slice_fusion
  61.0 0.0 copy-start.3
  61.0 4.7 %all-to-all-start = ((bf16[8,1,512,256]{3,2,1,0:T(8,128)(2,1)}), bf16[8,1,512,256]{3,2,1,0:T(8,128)(2,1)}, u32[]{:S(2)}, u32[]{:S(2)}) async-start(bf16[8,1,512,256]{3,2,1,0:T(8,128)(2,1)} %constant_dynamic-update-slice_fusion), calls=%async_computation | async-start | bytes 4194304 | tf_op jit(solution)/shard_map/all_to_all | solution.py:46
  65.8 0.0 copy-done.3
  65.8 0.0 copy-start.4
  65.8 1.8 copy.60
  67.6 0.6 compare_reduce_fusion.2
  68.3 0.7 compare_reduce_fusion
  69.0 0.0 copy-done.4
  69.0 0.2 convert_reduce_fusion
  69.2 0.1 broadcast_bitcast_fusion
  69.2 1.8 broadcast_multiply_fusion.2
  71.0 43.9 %all-to-all-done = bf16[8,1,512,256]{3,2,1,0:T(8,128)(2,1)} async-done(((bf16[8,1,512,256]{3,2,1,0:T(8,128)(2,1)}), bf16[8,1,512,256]{3,2,1,0:T(8,128)(2,1)}, u32[]{:S(2)}, u32[]{:S(2)}) %all-to-all-start) | async-done | bytes 2097184 | tf_op jit(solution)/shard_map/all_to_all | solution.py:46
  114.9 3.5 %fusion.8 = f32[512,512]{1,0:T(8,128)S(1)} fusion(bf16[8,1,512,256]{3,2,1,0:T(8,128)(2,1)} %all-to-all-done), kind=kOutput, calls=%fused_computation.10 | convolution fusion | flops 1073741824 | bytes 3145728 | tf_op jit(solution)/shard_map/dot_general | solution.py:17
  118.4 4.5 %gather_fusion = f32[512]{0:T(512)S(1)} fusion(f32[512,512]{1,0:T(8,128)S(1)} %fusion.8, s32[512]{0:T(512)S(1)} %bitcast.63), kind=kCustom, calls=%fused_computation | custom fusion | bytes 8192 | tf_op jit(solution)/shard_map/jit(diagonal)/cond/branch_0_fun/gather | solution.py:53
  122.9 0.1 subtract_add_fusion
  123.0 3.9 %copy.65 = bf16[1,512,8,256]{1,3,2,0:T(8,128)(2,1)} copy(bf16[1,512,8,256]{3,1,2,0:T(8,128)(2,1)} %bitcast.10) | data formatting | bytes 4194304 | tf_op jit(solution)/shard_map/reshape | solution.py:45
  126.9 5.2 %convolution_bitcast_fusion = f32[1024,512]{0,1:T(8,128)S(1)} fusion(bf16[512,2048]{0,1:T(8,128)(2,1)} %bitcast.65, bf16[1024,2048]{1,0:T(8,128)(2,1)} %bitcast.82), kind=kOutput, calls=%fused_computation.9 | convolution fusion | flops 2147483648 | bytes 8388608 | tf_op jit(solution)/shard_map/dot_general | solution.py:14
  132.2 0.0 copy-start.1
  132.2 2.1 fusion.40
  134.3 2.1 fusion.36
  136.5 2.1 fusion.32
  138.6 0.0 copy-done.1
  138.6 1.5 fusion.28
  140.1 0.2 multiply_reduce_fusion.1
  140.4 0.3 fusion.64
  140.6 37.1 %psum.14 = f32[32,128]{1,0:T(8,128)S(1)} all-reduce(f32[32,128]{1,0:T(8,128)S(1)} %fusion.64), channel_id=1, replica_groups=mesh['py'=4,'px'=8] {'py','px'}, use_global_device_ids=true, to_apply=%region_5.6 | all-reduce | flops 4096 | bytes 32768 | tf_op jit(solution)/shard_map/psum | solution.py:68
  177.8 0.2 convolution_bitcast_fusion.2
  177.9 0.0 copy-start.2
  177.9 0.2 broadcast_multiply_fusion.1
  178.2 1.4 copy-done.2
  179.6 2.1 fusion.25
  181.7 2.1 fusion.21
  183.8 2.0 fusion.17
  185.9 1.4 fusion.13
  187.4 0.0 copy-start
  187.4 1.3 copy-done
  188.7 0.2 multiply_reduce_fusion
  188.9 0.3 fusion.62
  189.2 42.4 %psum.15 = f32[32,128]{1,0:T(8,128)S(1)} all-reduce(f32[32,128]{1,0:T(8,128)S(1)} %fusion.62), channel_id=1, replica_groups=mesh['py'=4,'px'=8] {'py','px'}, use_global_device_ids=true, to_apply=%region_7.8 | all-reduce | flops 4096 | bytes 32768 | tf_op jit(solution)/shard_map/psum | solution.py:68
  231.6 0.2 convolution_bitcast_fusion.1
  231.8 1.8 broadcast_multiply_fusion
  233.6 1.8 copy.74
  (18 shorter events, 0.6 us)
Async XLA Ops:
  6.5 40.6 %all-gather.2.cloned.1.call-start = ((), (), s32[]{:S(2)}) async-start(), calls=%async_computation.1 | async-start | bytes 2621440 | tf_op jit(solution)/shard_map/all_gather | solution.py:32
  61.0 4.7 %copy-start.3 = (f32[64,16,512]{2,1,0:T(8,128)S(1)}, f32[64,16,512]{2,1,0:T(8,128)}, u32[]{:S(2)}) copy-start(f32[64,16,512]{2,1,0:T(8,128)} %param.22) | copy-start | bytes 6291460
  61.0 53.9 %all-to-all-start = ((bf16[8,1,512,256]{3,2,1,0:T(8,128)(2,1)}), bf16[8,1,512,256]{3,2,1,0:T(8,128)(2,1)}, u32[]{:S(2)}, u32[]{:S(2)}) async-start(bf16[8,1,512,256]{3,2,1,0:T(8,128)(2,1)} %constant_dynamic-update-slice_fusion), calls=%async_computation | async-start | bytes 4194304 | tf_op jit(solution)/shard_map/all_to_all | solution.py:46
  65.8 3.2 %copy-start.4 = (s32[1,1,4]{2,1,0:T(1,128)S(1)}, s32[1,1,4]{2,1,0:T(1,128)}, u32[]{:S(2)}) copy-start(s32[1,1,4]{2,1,0:T(1,128)} %param.23) | copy-start | bytes 52
  132.2 6.5 %copy-start.1 = (f32[1024,512]{0,1:T(8,128)}, f32[1024,512]{0,1:T(8,128)S(1)}, u32[]{:S(2)}) copy-start(f32[1024,512]{0,1:T(8,128)S(1)} %convolution_bitcast_fusion) | copy-start | bytes 6291460
  177.9 1.6 copy-start.2
  187.4 1.3 copy-start
Sparse Core Ops, SparseCore 0:
  9.2 37.8 all-gather.1
